TPU v7x, 32 devices: a whole 2x2x4 slice. The times are simulated.
32 devices in a mesh: row: 8 (over y, x, core), col: 4 (over z).
Axes of the slice: x: 2, y: 2, z: 4, core: 2. Of those that a mesh axis runs over, the one named last changes fastest.
Arguments:
- left_factors: float32 [128, 256, 32], P(None, ('row', 'col')), may hold values from -12 to 12
- right_factors: float32 [128, 128, 32], P(None, ('col', 'row')), may hold values from -12 to 12
- weight: float32 [1024, 128], replicated, may hold values from -0.1875 to 0.1875
- bias: float32 [128], replicated, may hold values from -2 to 2
- cotangent: float32 [256, 128, 128], P('row', 'col'), may hold values from -6 to 6
Outputs:
- pair_out: float32 [256, 128, 128], P('row', 'col')
- left_grad: float32 [128, 256, 32], P(None, ('row', 'col'))
- right_grad: float32 [128, 128, 32], P(None, ('col', 'row'))
- weight_grad: float32 [1024, 128], replicated
- bias_grad: float32 [128], replicated
All inputs are finite; a program needn't handle non-finite values.
Results may differ from a plain program's by a relative error of at most 0.0001.
Values sent between devices are 32-bit elements; how exact they have to be, the bound alone decides.
A program may use at most 64 MiB of HBM per device.

v0:
```python
import jax
import jax.numpy as jnp
from jax import lax
from jax.sharding import PartitionSpec as P


def per_device(left_factors, right_factors, weight, bias, cotangent):
    high = lax.Precision.HIGHEST
    samples = left_factors.shape[0]
    width = left_factors.shape[2]
    pair_width = weight.shape[1]
    left_all = lax.all_gather(left_factors, "col", axis=1, tiled=True)
    right_all = lax.all_gather(right_factors, "row", axis=1, tiled=True)
    tile_rows = left_all.shape[1]
    tile_cols = right_all.shape[1]
    step_rows = 16
    blocks = tile_rows // step_rows
    left_blocks = left_all.reshape(samples, blocks, step_rows, width).transpose(1, 0, 2, 3)
    cot_blocks = cotangent.reshape(blocks, step_rows, tile_cols, pair_width)

    def visit(carry, item):
        weight_sum, right_sum = carry
        left_block, cot_block = item
        outer = jnp.einsum("sic,sjd->ijcd", left_block, right_all, precision=high) / samples
        flat = outer.reshape(step_rows, tile_cols, width * width)
        pair_block = jnp.einsum("ijk,ke->ije", flat, weight, precision=high) + bias
        grad_flat = jnp.einsum("ije,ke->ijk", cot_block, weight, precision=high)
        weight_sum = weight_sum + jnp.einsum("ijk,ije->ke", flat, cot_block, precision=high)
        grad_outer = grad_flat.reshape(step_rows, tile_cols, width, width)
        left_block_grad = (
            jnp.einsum("ijcd,sjd->sic", grad_outer, right_all, precision=high) / samples
        )
        right_sum = (
            right_sum
            + jnp.einsum("ijcd,sic->sjd", grad_outer, left_block, precision=high) / samples
        )
        return ((weight_sum, right_sum), (pair_block, left_block_grad))

    start = (
        jnp.zeros((width * width, pair_width), jnp.float32),
        jnp.zeros((samples, tile_cols, width), jnp.float32),
    )
    (weight_part, right_part), (pair_blocks, left_pieces) = lax.scan(
        visit, start, (left_blocks, cot_blocks)
    )
    pair_out = pair_blocks.reshape(tile_rows, tile_cols, pair_width)
    left_part = left_pieces.transpose(1, 0, 2, 3).reshape(samples, tile_rows, width)
    bias_part = jnp.sum(cotangent, axis=(0, 1))
    left_total = lax.psum(left_part, "col")
    right_total = lax.psum(right_part, "row")
    left_share = tile_rows // lax.axis_size("col")
    right_share = tile_cols // lax.axis_size("row")
    left_grad = lax.dynamic_slice_in_dim(
        left_total, lax.axis_index("col") * left_share, left_share, 1
    )
    right_grad = lax.dynamic_slice_in_dim(
        right_total, lax.axis_index("row") * right_share, right_share, 1
    )
    weight_half, bias_half = lax.psum((weight_part, bias_part), "col")
    weight_total, bias_total = lax.psum((weight_half, bias_half), "row")
    total_rows = tile_rows * lax.axis_size("row")
    weight_grad = weight_total / total_rows
    bias_grad = bias_total / total_rows
    return (pair_out, left_grad, right_grad, weight_grad, bias_grad)


def solution(mesh):
    in_specs = (
        P(None, ("row", "col"), None),
        P(None, ("col", "row"), None),
        P(),
        P(),
        P("row", "col", None),
    )
    out_specs = (
        P("row", "col", None),
        P(None, ("row", "col"), None),
        P(None, ("col", "row"), None),
        P(),
        P(),
    )
    return jax.shard_map(
        per_device, mesh=mesh, in_specs=in_specs, out_specs=out_specs, check_vma=False
    )
```

profile of v0, /device:TPU:0, one launch (start us, length us, event | category | flops | bytes accessed | tf_op | source)
XLA Modules:
  0.0 329.0 jit_solution(1549016555022079670)
XLA Ops:
  7.2 0.0 all-reduce.7.cloned.1.call-start
  7.2 11.6 %all_gather.7 = f32[128,32,32]{0,2,1:T(8,128)S(1)} all-gather(f32[128,4,32]{0,2,1:T(8,128)} %param.8), channel_id=1, replica_groups=mesh['row'=8,'col'=4] {'row'}, dimensions={1}, use_global_device_ids=true | all-gather | bytes 589824 | tf_op jit(solution)/shard_map/all_gather | solution.py:13
  18.9 0.3 copy.17
  19.2 16.6 %all_gather.6 = f32[128,32,32]{0,2,1:T(8,128)S(1)} all-gather(f32[128,8,32]{0,2,1:T(8,128)} %param.7), channel_id=1, replica_groups=mesh['row'=8,'col'=4] {'col'}, dimensions={1}, use_global_device_ids=true | all-gather | bytes 655360 | tf_op jit(solution)/shard_map/all_gather | solution.py:12
  35.7 170.8 %while.17 = (s32[]{:T(128)}, f32[1024,128]{1,0:T(8,128)}, f32[128,32,32]{0,2,1:T(8,128)}, f32[2,16,32,128]{3,2,1,0:T(8,128)}, f32[2,128,16,32]{1,3,2,0:T(8,128)}...) while((s32[]{:T(128)}, f32[1024,128]{1,0:T(8,128)}, ...), condition=%wide.region_1.2_spmd.clone, body=%wide.region_0.1_spmd.clone.sunk | while | flops 4833148928 | bytes 49812356 | solution.py:43
  59.1 0.0 copy-start.2
  59.1 0.8 copy-done.2
  59.9 9.1 %multiply_bitcast_fusion.2 = f32[16,32,32,32]{3,2,1,0:T(8,128)} fusion(f32[128,32,32]{0,1,2:T(8,128)S(1)} %get-tuple-element.222, f32[2,128,16,32]{1,3,2,0:T(8,128)S(1)} %get-tuple-element.221, s32[]{:T(128)} %get-tuple-element.204), kind=kOutput, calls=%fused_computation.2.clone.1 | convolution fusion | flops 805830656 | bytes 2883588 | tf_op jit(solution)/shard_map/while/body/eval_jaxpr/sic,sjd->ijcd/dot_general | solution.py:24
  68.9 0.0 copy-start.1
  68.9 6.7 %reshape.43 = f32[16,32,1024]{2,1,0:T(8,128)S(1)} reshape(f32[16,32,32,32]{3,2,1,0:T(8,128)} %multiply_bitcast_fusion.2) | data formatting | bytes 4194304 | tf_op jit(solution)/shard_map/while/body/eval_jaxpr/reshape | solution.py:25
  75.6 0.0 copy-start.4
  75.7 5.2 %fusion.67 = f32[1024,128]{1,0:T(8,128)} fusion(f32[16,32,1024]{2,1,0:T(8,128)S(1)} %reshape.43, f32[1024,128]{1,0:T(8,128)} %get-tuple-element.205, pred[]{:T(512)S(6)} %compare.3, f32[2,16,32,128]{3,2,1,0:T(8,128)} %get-tuple-element.223, s32[]{:T(128)} %get-tuple-element.204), kind=kOutput, calls=%fused_computation.5.clone.1 | convolution fusion | flops 805568512 | bytes 3408385 | tf_op jit(solution)/shard_map/while/body/eval_jaxpr/ijk,ije->ke/dot_general | solution.py:28
  80.9 0.0 copy-done.1
  80.9 0.0 copy-start.8
  80.9 7.7 %fusion.68 = f32[16,32,32,32]{3,1,2,0:T(8,128)S(1)} fusion(f32[32,32,128,1]{2,1,0,3:T(8,128)S(1)} %bitcast.110, f32[2,16,32,128]{3,2,1,0:T(8,128)} %get-tuple-element.223, s32[]{:T(128)} %get-tuple-element.204), kind=kOutput, calls=%fused_computation.19.clone.1 | convolution fusion | flops 805306368 | bytes 2884096 | tf_op jit(solution)/shard_map/while/body/eval_jaxpr/ije,ke->ijk/dot_general | solution.py:27
  88.6 0.0 copy-start
  88.6 3.2 copy-done
  91.8 0.0 copy-done.4
  91.8 17.0 %fusion.69 = f32[128,32,32]{0,2,1:T(8,128)S(1)} fusion(f32[16,32,32,32]{3,1,2,0:T(8,128)S(1)} %fusion.68, f32[128,32,32]{0,2,1:T(8,128)S(1)} %copy-done.4, pred[]{:T(512)S(6)} %compare.3, f32[2,128,16,32]{1,3,2,0:T(8,128)} %copy-done.2, s32[]{:T(128)} %get-tuple-element.204), kind=kOutput, calls=%fused_computation.7.clone.1 | convolution fusion | flops 805699584 | bytes 3408385 | tf_op jit(solution)/shard_map/while/body/eval_jaxpr/ijcd,sic->sjd/dot_general | solution.py:35
  108.8 0.0 copy-start.5
  108.8 0.8 copy-done.5
  109.5 0.0 copy-done.8
  109.6 2.5 fusion.70
  112.1 0.0 copy-start.6
  112.1 10.6 %copy.39 = f32[16,32,32,32]{1,2,3,0:T(8,128)} copy(f32[16,32,32,32]{3,1,2,0:T(8,128)} %copy-done) | data formatting | bytes 4194304 | tf_op jit(solution)/shard_map/while/body/eval_jaxpr/ije,ke->ijk/dot_general | solution.py:27
  122.7 0.0 copy-done.6
  122.7 9.2 %fusion.71 = f32[2,128,16,32]{1,3,2,0:T(8,128)S(1)} fusion(f32[2,128,16,32]{1,3,2,0:T(8,128)S(1)} %copy-done.6, s32[]{:T(128)} %get-tuple-element.204, f32[16,32,32,32]{1,2,3,0:T(8,128)} %copy.39, f32[128,32,32]{0,1,2:T(8,128)S(1)} %get-tuple-element.222), kind=kOutput, calls=%fused_computation.14.clone.1 | convolution fusion | flops 805371904 | bytes 2883588 | tf_op jit(solution)/shard_map/while/body/eval_jaxpr/ijcd,sjd->sic/dot_general | solution.py:31
  131.9 0.0 copy-start.7
  131.9 0.8 copy-done.7
  132.7 0.0 copy-done.3
  132.7 0.0 copy-start.2
  132.7 0.8 copy-done.2
  133.5 9.0 %multiply_bitcast_fusion.2 = f32[16,32,32,32]{3,2,1,0:T(8,128)} fusion(f32[128,32,32]{0,1,2:T(8,128)S(1)} %get-tuple-element.222, f32[2,128,16,32]{1,3,2,0:T(8,128)S(1)} %get-tuple-element.221, s32[]{:T(128)} %get-tuple-element.204), kind=kOutput, calls=%fused_computation.2.clone.1 | convolution fusion | flops 805830656 | bytes 2883588 | tf_op jit(solution)/shard_map/while/body/eval_jaxpr/sic,sjd->ijcd/dot_general | solution.py:24
  142.6 6.7 %reshape.43 = f32[16,32,1024]{2,1,0:T(8,128)S(1)} reshape(f32[16,32,32,32]{3,2,1,0:T(8,128)} %multiply_bitcast_fusion.2) | data formatting | bytes 4194304 | tf_op jit(solution)/shard_map/while/body/eval_jaxpr/reshape | solution.py:25
  149.3 0.0 copy-start.4
  149.3 5.4 %fusion.67 = f32[1024,128]{1,0:T(8,128)} fusion(f32[16,32,1024]{2,1,0:T(8,128)S(1)} %reshape.43, f32[1024,128]{1,0:T(8,128)} %get-tuple-element.205, pred[]{:T(512)S(6)} %compare.3, f32[2,16,32,128]{3,2,1,0:T(8,128)} %get-tuple-element.223, s32[]{:T(128)} %get-tuple-element.204), kind=kOutput, calls=%fused_computation.5.clone.1 | convolution fusion | flops 805568512 | bytes 3408385 | tf_op jit(solution)/shard_map/while/body/eval_jaxpr/ijk,ije->ke/dot_general | solution.py:28
  154.7 0.0 copy-done.1
  154.7 7.7 %fusion.68 = f32[16,32,32,32]{3,1,2,0:T(8,128)S(1)} fusion(f32[32,32,128,1]{2,1,0,3:T(8,128)S(1)} %bitcast.110, f32[2,16,32,128]{3,2,1,0:T(8,128)} %get-tuple-element.223, s32[]{:T(128)} %get-tuple-element.204), kind=kOutput, calls=%fused_computation.19.clone.1 | convolution fusion | flops 805306368 | bytes 2884096 | tf_op jit(solution)/shard_map/while/body/eval_jaxpr/ije,ke->ijk/dot_general | solution.py:27
  162.4 0.0 copy-start
  162.4 3.2 copy-done
  165.6 0.0 copy-done.4
  165.6 17.0 %fusion.69 = f32[128,32,32]{0,2,1:T(8,128)S(1)} fusion(f32[16,32,32,32]{3,1,2,0:T(8,128)S(1)} %fusion.68, f32[128,32,32]{0,2,1:T(8,128)S(1)} %copy-done.4, pred[]{:T(512)S(6)} %compare.3, f32[2,128,16,32]{1,3,2,0:T(8,128)} %copy-done.2, s32[]{:T(128)} %get-tuple-element.204), kind=kOutput, calls=%fused_computation.7.clone.1 | convolution fusion | flops 805699584 | bytes 3408385 | tf_op jit(solution)/shard_map/while/body/eval_jaxpr/ijcd,sic->sjd/dot_general | solution.py:35
  182.6 0.0 copy-start.5
  182.6 0.8 copy-done.5
  183.4 0.0 copy-done.8
  183.4 2.5 fusion.70
  185.9 10.6 %copy.39 = f32[16,32,32,32]{1,2,3,0:T(8,128)} copy(f32[16,32,32,32]{3,1,2,0:T(8,128)} %copy-done) | data formatting | bytes 4194304 | tf_op jit(solution)/shard_map/while/body/eval_jaxpr/ije,ke->ijk/dot_general | solution.py:27
  196.5 0.0 copy-done.6
  196.5 9.2 %fusion.71 = f32[2,128,16,32]{1,3,2,0:T(8,128)S(1)} fusion(f32[2,128,16,32]{1,3,2,0:T(8,128)S(1)} %copy-done.6, s32[]{:T(128)} %get-tuple-element.204, f32[16,32,32,32]{1,2,3,0:T(8,128)} %copy.39, f32[128,32,32]{0,1,2:T(8,128)S(1)} %get-tuple-element.222), kind=kOutput, calls=%fused_computation.14.clone.1 | convolution fusion | flops 805371904 | bytes 2883588 | tf_op jit(solution)/shard_map/while/body/eval_jaxpr/ijcd,sjd->sic/dot_general | solution.py:31
  205.7 0.0 copy-start.7
  205.7 0.8 copy-done.7
  206.5 0.0 copy-done.3
  206.5 0.0 all-reduce.7.cloned.1.call-update
  206.6 0.0 all-reduce.5.cloned.1.call-start
  206.6 52.6 %all-reduce.7.cloned.1.call-done = (f32[128,32,32]{0,2,1:T(8,128)}, f32[1024,128]{1,0:T(8,128)}) async-done(((f32[128,32,32]{0,2,1:T(8,128)}, f32[1024,128]{1,0:T(8,128)}), (f32[128,32,32]{0,2,1:T(8,128)}, f32[1024,128]{1,0:T(8,128)})) %all-reduce.7.cloned.1.call-update) | async-done | bytes 1048592 | tf_op jit(solution)/shard_map/psum | solution.py:49
  259.2 0.0 all-reduce.5.cloned.1.call-update
  259.2 1.2 reduce_sum.9
  260.4 10.0 %psum.46 = f32[128]{0:T(128)S(1)} all-reduce(f32[128]{0:T(128)S(1)} %reduce_sum.9), channel_id=1, replica_groups=mesh['row'=8,'col'=4] {'col'}, use_global_device_ids=true, to_apply=%region_7.8 | all-reduce | flops 128 | bytes 1024 | tf_op jit(solution)/shard_map/psum | solution.py:59
  270.4 11.8 %psum.47 = f32[128]{0:T(128)S(1)} all-reduce(f32[128]{0:T(128)S(1)} %psum.46), channel_id=1, replica_groups=mesh['row'=8,'col'=4] {'row'}, use_global_device_ids=true, to_apply=%region_8.9 | all-reduce | flops 128 | bytes 1024 | tf_op jit(solution)/shard_map/psum | solution.py:60
  282.3 0.5 broadcast_multiply_fusion.1
  282.8 1.6 constant_dynamic-slice_fusion.1
  284.4 34.1 %all-reduce.5.cloned.1.call-done = (f32[128,32,32]{0,2,1:T(8,128)}, f32[1024,128]{1,0:T(8,128)}) async-done(((f32[128,32,32]{0,2,1:T(8,128)}, f32[1024,128]{1,0:T(8,128)}), (f32[128,32,32]{0,2,1:T(8,128)}, f32[1024,128]{1,0:T(8,128)})) %all-reduce.5.cloned.1.call-update) | async-done | bytes 1048592 | tf_op jit(solution)/shard_map/psum | solution.py:50
  318.5 1.9 broadcast_multiply_fusion
  320.3 1.5 constant_dynamic-slice_fusion
  (9 shorter events, 0.0 us)
Async XLA Ops:
  7.2 252.0 %all-reduce.7.cloned.1.call-start = ((), (), s32[]{:S(2)}) async-start(), calls=%async_computation.1 | async-start | bytes 2097152 | tf_op jit(solution)/shard_map/psum | solution.py:49
  59.1 0.8 copy-start.2
  68.9 12.0 %copy-start.1 = (f32[1024,128]{1,0:T(8,128)S(1)}, f32[1024,128]{1,0:T(8,128)}, u32[]{:S(2)}) copy-start(f32[1024,128]{1,0:T(8,128)} %get-tuple-element.224) | copy-start | bytes 1572868 | tf_op jit(solution)/shard_map/while
  75.6 16.1 %copy-start.4 = (f32[128,32,32]{0,2,1:T(8,128)S(1)}, f32[128,32,32]{0,2,1:T(8,128)}, u32[]{:S(2)}) copy-start(f32[128,32,32]{0,2,1:T(8,128)} %get-tuple-element.206) | copy-start | bytes 1572868 | tf_op jit(solution)/shard_map/while
  80.9 28.7 %copy-start.8 = (f32[128]{0:T(128)S(1)}, f32[128]{0:T(128)}, u32[]{:S(2)}) copy-start(f32[128]{0:T(128)} %get-tuple-element.225) | copy-start | bytes 1540 | tf_op jit(solution)/shard_map/while
  88.6 3.2 copy-start
  108.8 0.8 copy-start.5
  112.1 10.6 %copy-start.6 = (f32[2,128,16,32]{1,3,2,0:T(8,128)S(1)}, f32[2,128,16,32]{1,3,2,0:T(8,128)}, u32[]{:S(2)}) copy-start(f32[2,128,16,32]{1,3,2,0:T(8,128)} %get-tuple-element.208) | copy-start | bytes 1572868 | tf_op jit(solution)/shard_map/while
  122.7 10.0 %copy-start.3 = (f32[2,128,16,32]{1,3,2,0:T(8,128)S(1)}, f32[2,128,16,32]{1,3,2,0:T(8,128)}, u32[]{:S(2)}) copy-start(f32[2,128,16,32]{1,3,2,0:T(8,128)} %copy-done.2) | copy-start | bytes 1572868 | tf_op jit(solution)/shard_map/while
  131.9 0.8 copy-start.7
  132.7 0.8 copy-start.2
  142.6 12.1 %copy-start.1 = (f32[1024,128]{1,0:T(8,128)S(1)}, f32[1024,128]{1,0:T(8,128)}, u32[]{:S(2)}) copy-start(f32[1024,128]{1,0:T(8,128)} %get-tuple-element.224) | copy-start | bytes 1572868 | tf_op jit(solution)/shard_map/while
  149.3 16.3 %copy-start.4 = (f32[128,32,32]{0,2,1:T(8,128)S(1)}, f32[128,32,32]{0,2,1:T(8,128)}, u32[]{:S(2)}) copy-start(f32[128,32,32]{0,2,1:T(8,128)} %get-tuple-element.206) | copy-start | bytes 1572868 | tf_op jit(solution)/shard_map/while
  154.7 28.7 %copy-start.8 = (f32[128]{0:T(128)S(1)}, f32[128]{0:T(128)}, u32[]{:S(2)}) copy-start(f32[128]{0:T(128)} %get-tuple-element.225) | copy-start | bytes 1540 | tf_op jit(solution)/shard_map/while
  162.4 3.2 copy-start
  182.6 0.8 copy-start.5
  185.9 10.6 %copy-start.6 = (f32[2,128,16,32]{1,3,2,0:T(8,128)S(1)}, f32[2,128,16,32]{1,3,2,0:T(8,128)}, u32[]{:S(2)}) copy-start(f32[2,128,16,32]{1,3,2,0:T(8,128)} %get-tuple-element.208) | copy-start | bytes 1572868 | tf_op jit(solution)/shard_map/while
  196.5 10.0 %copy-start.3 = (f32[2,128,16,32]{1,3,2,0:T(8,128)S(1)}, f32[2,128,16,32]{1,3,2,0:T(8,128)}, u32[]{:S(2)}) copy-start(f32[2,128,16,32]{1,3,2,0:T(8,128)} %copy-done.2) | copy-start | bytes 1572868 | tf_op jit(solution)/shard_map/while
  205.7 0.8 copy-start.7
  206.6 111.9 %all-reduce.5.cloned.1.call-start = ((), (), s32[]{:S(2)}) async-start(), calls=%async_computation | async-start | bytes 2097152 | tf_op jit(solution)/shard_map/psum | solution.py:50
Sparse Core Ops, SparseCore 0:
  206.7 52.4 all-reduce.6
  262.4 56.0 all-reduce.4
where the time goes:
time: 332 us; the launch traced here: 329 us
  matrix products  101 us (30%)
  waiting for transfers between devices  86.7 us (26%)
  blocking collectives  50 us (15%)
  local copies, waits for them, and re-layouts  49.2 us (15%)
  loops' own time  23.5 us (7%)
  between operations  14.5 us (4%)
  other arithmetic  3.58 us (1%)
    psum x1, waiting for transfers between devices, per_device(): left_total = lax.psum(left_part, 'col')  52.6 us
    psum x1, waiting for transfers between devices, per_device(): right_total = lax.psum(right_part, 'row')  34.1 us
    dot_general x2, matrix products, visit(): jnp.einsum('ijcd,sic->sjd', grad_outer, left_block, precision=high)  33.9 us
    another operation x1, loops' own time, per_device(): lax.scan(visit, start, (left_blocks, cot_blocks))  23.5 us
    dot_general x2, local copies, waits for them, and re-layouts, visit(): grad_flat = jnp.einsum('ije,ke->ijk', cot_block, weight, precision=high)  21.3 us
    dot_general x2, matrix products, visit(): jnp.einsum('ijcd,sjd->sic', grad_outer, right_all, precision=high) / samples  18.4 us
    dot_general x2, matrix products, visit(): jnp.einsum('sic,sjd->ijcd', left_block, right_all, precision=high) / samples  18.1 us
    all_gather x1, blocking collectives, per_device(): left_all = lax.all_gather(left_factors, 'col', axis=1, tiled=True)  16.6 us
  transfers between devices with their start and end apart: 2, of which 2 were waited for; matrix products, arithmetic and copies ran while one was open for 1% of the time, Pallas kernels for 0%

commit v1 on v0

--- a/solution.py
+++ b/solution.py
@@ -47,7 +47,7 @@
     left_part = left_pieces.transpose(1, 0, 2, 3).reshape(samples, tile_rows, width)
     bias_part = jnp.sum(cotangent, axis=(0, 1))
     left_total = lax.psum(left_part, "col")
-    right_total = lax.psum(right_part, "row")
+    right_total = jnp.sum(lax.all_gather(right_part, "row"), axis=0)
     left_share = tile_rows // lax.axis_size("col")
     right_share = tile_cols // lax.axis_size("row")
     left_grad = lax.dynamic_slice_in_dim(

time: 332 us -> 374 us (1.13)
  waiting for transfers between devices: 86.7 us -> 122 us
  local copies, waits for them, and re-layouts: 49.2 us -> 53.6 us
    all_gather x0 -> x1, waiting for transfers between devices: none -> 36.7 us  [per_device(): right_total = jnp.sum(lax.all_gather(right_part, 'row'), axis=0)]
    unnamed x1 -> x2, local copies, waits for them, and re-layouts: 0.31 us -> 5.48 us
    while x36 -> x44, local copies, waits for them, and re-layouts: 11.2 us -> 11.3 us
  transfers between devices with their start and end apart: 2 -> 3, of which waited for: 2 -> 3; matrix products, arithmetic and copies ran while one was open for 1% -> 1% of each run, Pallas kernels for 0% -> 0%
where the time goes in v1:
time: 374 us; the launch traced here: 372 us
  waiting for transfers between devices  122 us (33%)
  matrix products  100 us (27%)
  local copies, waits for them, and re-layouts  53.6 us (14%)
  blocking collectives  49.5 us (13%)
  loops' own time  26.2 us (7%)
  between operations  14 us (4%)
  other arithmetic  6.77 us (2%)
    psum x1, waiting for transfers between devices, per_device(): left_total = lax.psum(left_part, 'col')  52.8 us
    all_gather x1, waiting for transfers between devices, per_device(): right_total = jnp.sum(lax.all_gather(right_part, 'row'), axis=0)  36.7 us
    dot_general x2, matrix products, visit(): jnp.einsum('ijcd,sic->sjd', grad_outer, left_block, precision=high)  33.9 us
    psum x1, waiting for transfers between devices, per_device(): weight_total, bias_total = lax.psum((weight_half, bias_half), 'row')  31.3 us
    another operation x1, loops' own time, per_device(): lax.scan(visit, start, (left_blocks, cot_blocks))  26.2 us
    dot_general x2, local copies, waits for them, and re-layouts, visit(): grad_flat = jnp.einsum('ije,ke->ijk', cot_block, weight, precision=high)  21.3 us
    dot_general x2, matrix products, visit(): jnp.einsum('ijcd,sjd->sic', grad_outer, right_all, precision=high) / samples  18.4 us
    dot_general x2, matrix products, visit(): jnp.einsum('sic,sjd->ijcd', left_block, right_all, precision=high) / samples  18.1 us
  transfers between devices with their start and end apart: 3, of which 3 were waited for; matrix products, arithmetic and copies ran while one was open for 1% of the time, Pallas kernels for 0%

profile of v1, /device:TPU:0, one launch (start us, length us, event | category | flops | bytes accessed | tf_op | source)
XLA Modules:
  0.0 371.9 jit_solution(4431208736060663664)
XLA Ops:
  7.2 0.0 all-reduce.6.cloned.1.call-start
  7.2 17.6 %all_gather.12 = f32[128,32,32]{0,2,1:T(8,128)S(1)} all-gather(f32[128,8,32]{0,2,1:T(8,128)} %param.7), channel_id=1, replica_groups=mesh['row'=8,'col'=4] {'col'}, dimensions={1}, use_global_device_ids=true | all-gather | bytes 655360 | tf_op jit(solution)/shard_map/all_gather | solution.py:12
  24.8 10.1 %all_gather.13 = f32[128,32,32]{0,2,1:T(8,128)S(1)} all-gather(f32[128,4,32]{0,2,1:T(8,128)} %param.8), channel_id=1, replica_groups=mesh['row'=8,'col'=4] {'row'}, dimensions={1}, use_global_device_ids=true | all-gather | bytes 589824 | tf_op jit(solution)/shard_map/all_gather | solution.py:13
  35.0 0.3 copy.17
  35.3 172.2 %while.17 = (s32[]{:T(128)}, f32[1024,128]{1,0:T(8,128)}, f32[128,32,32]{0,2,1:T(8,128)}, f32[2,16,32,128]{3,2,1,0:T(8,128)}, f32[2,128,16,32]{1,3,2,0:T(8,128)}...) while((s32[]{:T(128)}, f32[1024,128]{1,0:T(8,128)}, ...), condition=%wide.region_1.2_spmd.clone, body=%wide.region_0.1_spmd.clone.sunk | while | flops 4833148928 | bytes 54004692 | solution.py:43
  58.6 0.0 copy-start.2
  58.6 0.8 copy-done.2
  59.4 9.0 %multiply_bitcast_fusion.2 = f32[16,32,32,32]{3,2,1,0:T(8,128)} fusion(f32[128,32,32]{0,1,2:T(8,128)S(1)} %get-tuple-element.220, f32[2,128,16,32]{1,3,2,0:T(8,128)S(1)} %get-tuple-element.219, s32[]{:T(128)S(6)} %copy.49), kind=kOutput, calls=%fused_computation.2.clone.1 | convolution fusion | flops 805830656 | bytes 2883588 | tf_op jit(solution)/shard_map/while/body/eval_jaxpr/sic,sjd->ijcd/dot_general | solution.py:24
  68.4 6.7 %reshape.44 = f32[16,32,1024]{2,1,0:T(8,128)S(1)} reshape(f32[16,32,32,32]{3,2,1,0:T(8,128)} %multiply_bitcast_fusion.2) | data formatting | bytes 4194304 | tf_op jit(solution)/shard_map/while/body/eval_jaxpr/reshape | solution.py:25
  75.1 0.0 copy-start.4
  75.1 5.2 %fusion.67 = f32[1024,128]{1,0:T(8,128)} fusion(f32[16,32,1024]{2,1,0:T(8,128)S(1)} %reshape.44, f32[1024,128]{1,0:T(8,128)} %get-tuple-element.203, pred[]{:T(512)S(6)} %compare.3, f32[2,16,32,128]{3,2,1,0:T(8,128)} %get-tuple-element.221, s32[]{:T(128)S(6)} %copy.49), kind=kOutput, calls=%fused_computation.5.clone.1 | convolution fusion | flops 805568512 | bytes 3407877 | tf_op jit(solution)/shard_map/while/body/eval_jaxpr/ijk,ije->ke/dot_general | solution.py:28
  80.4 0.0 copy-done.1
  80.4 7.7 %fusion.68 = f32[16,32,32,32]{3,1,2,0:T(8,128)S(1)} fusion(f32[32,32,128,1]{2,1,0,3:T(8,128)S(1)} %bitcast.116, f32[2,16,32,128]{3,2,1,0:T(8,128)} %get-tuple-element.221, s32[]{:T(128)S(6)} %copy.49), kind=kOutput, calls=%fused_computation.19.clone.1 | convolution fusion | flops 805306368 | bytes 2883588 | tf_op jit(solution)/shard_map/while/body/eval_jaxpr/ije,ke->ijk/dot_general | solution.py:27
  88.1 0.0 copy-start
  88.1 3.2 copy-done
  91.3 0.0 copy-done.4
  91.3 17.0 %fusion.69 = f32[128,32,32]{0,2,1:T(8,128)S(1)} fusion(f32[16,32,32,32]{3,1,2,0:T(8,128)S(1)} %fusion.68, f32[128,32,32]{0,2,1:T(8,128)S(1)} %copy-done.4, pred[]{:T(512)S(6)} %compare.3, f32[2,128,16,32]{1,3,2,0:T(8,128)} %copy-done.2, s32[]{:T(128)S(6)} %copy.49), kind=kOutput, calls=%fused_computation.7.clone.1 | convolution fusion | flops 805699584 | bytes 3407877 | tf_op jit(solution)/shard_map/while/body/eval_jaxpr/ijcd,sic->sjd/dot_general | solution.py:35
  108.3 0.0 copy-start.5
  108.3 0.0 copy-done.8
  108.3 0.0 copy-done.9
  108.3 1.8 fusion.70
  110.1 0.0 copy-done.5
  110.2 0.0 copy-start.10
  110.2 0.8 copy-done.10
  111.0 10.6 %copy.41 = f32[16,32,32,32]{1,2,3,0:T(8,128)} copy(f32[16,32,32,32]{3,1,2,0:T(8,128)} %copy-done) | data formatting | bytes 4194304 | tf_op jit(solution)/shard_map/while/body/eval_jaxpr/ije,ke->ijk/dot_general | solution.py:27
  121.6 0.0 copy-done.6
  121.6 9.2 %fusion.71 = f32[2,128,16,32]{1,3,2,0:T(8,128)S(1)} fusion(f32[2,128,16,32]{1,3,2,0:T(8,128)S(1)} %copy-done.6, s32[]{:T(128)S(6)} %copy.49, f32[16,32,32,32]{1,2,3,0:T(8,128)} %copy.41, f32[128,32,32]{0,1,2:T(8,128)S(1)} %get-tuple-element.220), kind=kOutput, calls=%fused_computation.14.clone.1 | convolution fusion | flops 805371904 | bytes 2883588 | tf_op jit(solution)/shard_map/while/body/eval_jaxpr/ijcd,sjd->sic/dot_general | solution.py:31
  130.8 0.0 copy-start.7
  130.8 0.8 copy-done.7
  131.6 0.0 copy-done.3
  131.6 0.8 copy-done.2
  132.4 9.0 %multiply_bitcast_fusion.2 = f32[16,32,32,32]{3,2,1,0:T(8,128)} fusion(f32[128,32,32]{0,1,2:T(8,128)S(1)} %get-tuple-element.220, f32[2,128,16,32]{1,3,2,0:T(8,128)S(1)} %get-tuple-element.219, s32[]{:T(128)S(6)} %copy.49), kind=kOutput, calls=%fused_computation.2.clone.1 | convolution fusion | flops 805830656 | bytes 2883588 | tf_op jit(solution)/shard_map/while/body/eval_jaxpr/sic,sjd->ijcd/dot_general | solution.py:24
  141.5 6.7 %reshape.44 = f32[16,32,1024]{2,1,0:T(8,128)S(1)} reshape(f32[16,32,32,32]{3,2,1,0:T(8,128)} %multiply_bitcast_fusion.2) | data formatting | bytes 4194304 | tf_op jit(solution)/shard_map/while/body/eval_jaxpr/reshape | solution.py:25
  148.2 5.4 %fusion.67 = f32[1024,128]{1,0:T(8,128)} fusion(f32[16,32,1024]{2,1,0:T(8,128)S(1)} %reshape.44, f32[1024,128]{1,0:T(8,128)} %get-tuple-element.203, pred[]{:T(512)S(6)} %compare.3, f32[2,16,32,128]{3,2,1,0:T(8,128)} %get-tuple-element.221, s32[]{:T(128)S(6)} %copy.49), kind=kOutput, calls=%fused_computation.5.clone.1 | convolution fusion | flops 805568512 | bytes 3407877 | tf_op jit(solution)/shard_map/while/body/eval_jaxpr/ijk,ije->ke/dot_general | solution.py:28
  153.6 7.7 %fusion.68 = f32[16,32,32,32]{3,1,2,0:T(8,128)S(1)} fusion(f32[32,32,128,1]{2,1,0,3:T(8,128)S(1)} %bitcast.116, f32[2,16,32,128]{3,2,1,0:T(8,128)} %get-tuple-element.221, s32[]{:T(128)S(6)} %copy.49), kind=kOutput, calls=%fused_computation.19.clone.1 | convolution fusion | flops 805306368 | bytes 2883588 | tf_op jit(solution)/shard_map/while/body/eval_jaxpr/ije,ke->ijk/dot_general | solution.py:27
  161.3 3.2 copy-done
  164.5 17.0 %fusion.69 = f32[128,32,32]{0,2,1:T(8,128)S(1)} fusion(f32[16,32,32,32]{3,1,2,0:T(8,128)S(1)} %fusion.68, f32[128,32,32]{0,2,1:T(8,128)S(1)} %copy-done.4, pred[]{:T(512)S(6)} %compare.3, f32[2,128,16,32]{1,3,2,0:T(8,128)} %copy-done.2, s32[]{:T(128)S(6)} %copy.49), kind=kOutput, calls=%fused_computation.7.clone.1 | convolution fusion | flops 805699584 | bytes 3407877 | tf_op jit(solution)/shard_map/while/body/eval_jaxpr/ijcd,sic->sjd/dot_general | solution.py:35
  181.5 0.0 copy-start.5
  181.5 0.0 copy-done.8
  181.5 0.0 copy-done.9
  181.5 1.8 fusion.70
  183.4 0.0 copy-start.10
  183.4 0.8 copy-done.10
  184.2 10.6 %copy.41 = f32[16,32,32,32]{1,2,3,0:T(8,128)} copy(f32[16,32,32,32]{3,1,2,0:T(8,128)} %copy-done) | data formatting | bytes 4194304 | tf_op jit(solution)/shard_map/while/body/eval_jaxpr/ije,ke->ijk/dot_general | solution.py:27
  194.8 9.2 %fusion.71 = f32[2,128,16,32]{1,3,2,0:T(8,128)S(1)} fusion(f32[2,128,16,32]{1,3,2,0:T(8,128)S(1)} %copy-done.6, s32[]{:T(128)S(6)} %copy.49, f32[16,32,32,32]{1,2,3,0:T(8,128)} %copy.41, f32[128,32,32]{0,1,2:T(8,128)S(1)} %get-tuple-element.220), kind=kOutput, calls=%fused_computation.14.clone.1 | convolution fusion | flops 805371904 | bytes 2883588 | tf_op jit(solution)/shard_map/while/body/eval_jaxpr/ijcd,sjd->sic/dot_general | solution.py:31
  204.0 0.0 copy-start.7
  204.0 0.8 copy-done.7
  207.5 0.0 all-reduce.6.cloned.1.call-update
  207.5 0.0 all-reduce.4.cloned.1.call-start
  207.5 52.8 %all-reduce.6.cloned.1.call-done = (f32[128,32,32]{0,2,1:T(8,128)}, f32[1024,128]{1,0:T(8,128)}) async-done(((f32[128,32,32]{0,2,1:T(8,128)}, f32[1024,128]{1,0:T(8,128)}), (f32[128,32,32]{0,2,1:T(8,128)}, f32[1024,128]{1,0:T(8,128)})) %all-reduce.6.cloned.1.call-update) | async-done | bytes 1048592 | tf_op jit(solution)/shard_map/psum | solution.py:49
  260.4 0.0 all-reduce.4.cloned.1.call-update
  260.4 0.0 all-gather.3.cloned.1.call-start
  260.4 0.7 all-gather.3.cloned.1.call-update
  261.1 1.2 reduce_sum.19
  262.3 10.0 %psum.38 = f32[128]{0:T(128)S(1)} all-reduce(f32[128]{0:T(128)S(1)} %reduce_sum.19), channel_id=1, replica_groups=mesh['row'=8,'col'=4] {'col'}, use_global_device_ids=true, to_apply=%region_7.8 | all-reduce | flops 128 | bytes 1024 | tf_op jit(solution)/shard_map/psum | solution.py:59
  272.3 11.8 %psum.39 = f32[128]{0:T(128)S(1)} all-reduce(f32[128]{0:T(128)S(1)} %psum.38), channel_id=1, replica_groups=mesh['row'=8,'col'=4] {'row'}, use_global_device_ids=true, to_apply=%region_8.9 | all-reduce | flops 128 | bytes 1024 | tf_op jit(solution)/shard_map/psum | solution.py:60
  284.2 0.5 broadcast_multiply_fusion.1
  284.7 1.6 constant_dynamic-slice_fusion.1
  286.2 31.3 %all-reduce.4.cloned.1.call-done = f32[1024,128]{1,0:T(8,128)} async-done(((f32[1024,128]{1,0:T(8,128)}), f32[1024,128]{1,0:T(8,128)}) %all-reduce.4.cloned.1.call-update) | async-done | bytes 524304 | tf_op jit(solution)/shard_map/psum | solution.py:60
  317.6 1.9 broadcast_multiply_fusion
  319.4 36.7 %all-gather.3.cloned.1.call-done = f32[1024,32,32]{0,2,1:T(8,128)} async-done(((f32[128,32,32]{0,2,1:T(8,128)}), f32[1024,32,32]{0,2,1:T(8,128)}) %all-gather.3.cloned.1.call-update) | async-done | bytes 4194320 | tf_op jit(solution)/shard_map/all_gather | solution.py:50
  356.1 5.2 %copy.22 = f32[128,8,8,128]{3,2,1,0:T(8,128)} copy(f32[128,8,8,128]{3,1,2,0:T(8,128)} %bitcast.121) | data formatting | bytes 8388608
  361.3 3.2 reduce_sum.18
  364.5 0.6 constant_dynamic-slice_fusion
  (22 shorter events, 0.0 us)
Async XLA Ops:
  7.2 253.2 %all-reduce.6.cloned.1.call-start = ((), (), s32[]{:S(2)}) async-start(), calls=%async_computation.2 | async-start | bytes 2097152 | tf_op jit(solution)/shard_map/psum | solution.py:49
  58.6 0.8 copy-start.2
  68.4 12.0 %copy-start.1 = (f32[1024,128]{1,0:T(8,128)S(1)}, f32[1024,128]{1,0:T(8,128)}, u32[]{:S(2)}) copy-start(f32[1024,128]{1,0:T(8,128)} %get-tuple-element.222) | copy-start | bytes 1572868 | tf_op jit(solution)/shard_map/while
  75.1 16.2 %copy-start.4 = (f32[128,32,32]{0,2,1:T(8,128)S(1)}, f32[128,32,32]{0,2,1:T(8,128)}, u32[]{:S(2)}) copy-start(f32[128,32,32]{0,2,1:T(8,128)} %get-tuple-element.204) | copy-start | bytes 1572868 | tf_op jit(solution)/shard_map/while
  80.4 27.9 %copy-start.8 = (f32[128]{0:T(128)S(1)}, f32[128]{0:T(128)}, u32[]{:S(2)}) copy-start(f32[128]{0:T(128)} %get-tuple-element.223) | copy-start | bytes 1540 | tf_op jit(solution)/shard_map/while
  80.4 27.9 %copy-start.9 = (f32[2,16,32,128]{3,2,1,0:T(8,128)S(1)}, f32[2,16,32,128]{3,2,1,0:T(8,128)}, u32[]{:S(2)}) copy-start(f32[2,16,32,128]{3,2,1,0:T(8,128)} %get-tuple-element.205) | copy-start | bytes 1572868 | tf_op jit(solution)/shard_map/while
  88.1 3.2 copy-start
  108.3 1.8 copy-start.5
  110.2 0.8 copy-start.10
  110.9 10.6 %copy-start.6 = (f32[2,128,16,32]{1,3,2,0:T(8,128)S(1)}, f32[2,128,16,32]{1,3,2,0:T(8,128)}, u32[]{:S(2)}) copy-start(f32[2,128,16,32]{1,3,2,0:T(8,128)} %get-tuple-element.206) | copy-start | bytes 1572868 | tf_op jit(solution)/shard_map/while
  121.6 10.0 %copy-start.3 = (f32[2,128,16,32]{1,3,2,0:T(8,128)S(1)}, f32[2,128,16,32]{1,3,2,0:T(8,128)}, u32[]{:S(2)}) copy-start(f32[2,128,16,32]{1,3,2,0:T(8,128)} %copy-done.2) | copy-start | bytes 1572868 | tf_op jit(solution)/shard_map/while
  130.8 0.8 copy-start.7
  131.6 0.8 copy-start.2
  141.5 12.1 %copy-start.1 = (f32[1024,128]{1,0:T(8,128)S(1)}, f32[1024,128]{1,0:T(8,128)}, u32[]{:S(2)}) copy-start(f32[1024,128]{1,0:T(8,128)} %get-tuple-element.222) | copy-start | bytes 1572868 | tf_op jit(solution)/shard_map/while
  148.2 16.4 %copy-start.4 = (f32[128,32,32]{0,2,1:T(8,128)S(1)}, f32[128,32,32]{0,2,1:T(8,128)}, u32[]{:S(2)}) copy-start(f32[128,32,32]{0,2,1:T(8,128)} %get-tuple-element.204) | copy-start | bytes 1572868 | tf_op jit(solution)/shard_map/while
  153.6 27.9 %copy-start.8 = (f32[128]{0:T(128)S(1)}, f32[128]{0:T(128)}, u32[]{:S(2)}) copy-start(f32[128]{0:T(128)} %get-tuple-element.223) | copy-start | bytes 1540 | tf_op jit(solution)/shard_map/while
  153.6 27.9 %copy-start.9 = (f32[2,16,32,128]{3,2,1,0:T(8,128)S(1)}, f32[2,16,32,128]{3,2,1,0:T(8,128)}, u32[]{:S(2)}) copy-start(f32[2,16,32,128]{3,2,1,0:T(8,128)} %get-tuple-element.205) | copy-start | bytes 1572868 | tf_op jit(solution)/shard_map/while
  161.3 3.2 copy-start
  181.5 1.8 copy-start.5
  183.4 0.8 copy-start.10
  184.2 10.6 %copy-start.6 = (f32[2,128,16,32]{1,3,2,0:T(8,128)S(1)}, f32[2,128,16,32]{1,3,2,0:T(8,128)}, u32[]{:S(2)}) copy-start(f32[2,128,16,32]{1,3,2,0:T(8,128)} %get-tuple-element.206) | copy-start | bytes 1572868 | tf_op jit(solution)/shard_map/while
  194.8 10.0 %copy-start.3 = (f32[2,128,16,32]{1,3,2,0:T(8,128)S(1)}, f32[2,128,16,32]{1,3,2,0:T(8,128)}, u32[]{:S(2)}) copy-start(f32[2,128,16,32]{1,3,2,0:T(8,128)} %copy-done.2) | copy-start | bytes 1572868 | tf_op jit(solution)/shard_map/while
  204.0 0.8 copy-start.7
  207.5 110.1 %all-reduce.4.cloned.1.call-start = ((), (), s32[]{:S(2)}) async-start(), calls=%async_computation | async-start | bytes 1048576 | tf_op jit(solution)/shard_map/psum | solution.py:60
  260.4 95.7 %all-gather.3.cloned.1.call-start = ((), (), s32[]{:S(2)}) async-start(), calls=%async_computation.1 | async-start | bytes 4718592 | tf_op jit(solution)/shard_map/all_gather | solution.py:50
Sparse Core Ops, SparseCore 0:
  207.6 52.7 all-reduce.5
  263.5 54.0 all-reduce.3
  319.4 36.6 all-gather.2
